TPU v7x, 32 devices: a whole 2x2x4 slice. The times are simulated.
32 devices in a mesh: batch: 4 (over y, core), proto: 8 (over z, x).
Axes of the slice: x: 2, y: 2, z: 4, core: 2. Of those that a mesh axis runs over, the one named last changes fastest.
Arguments:
- features: bfloat16 [4096, 256], P(('batch', 'proto')), may hold values from -8 to 8
- head_weight: bfloat16 [256, 65536], P('batch', 'proto'), may hold values from -0.375 to 0.375
- student_scores: bfloat16 [2, 4096, 65536], P(None, 'batch', 'proto'), may hold values from -1 to 1
Outputs:
- targets: bfloat16 [4096, 65536], P('batch', 'proto')
- row_loss: float32 [2, 4096], P(None, 'batch')
All inputs are finite; a program needn't handle non-finite values.
Results may differ from a plain program's by a relative error of at most 0.0013.
Values may be sent and summed in bfloat16 or wider, within the bound.
No kernel may reach another device: no remote copies, remote signals or barrier semaphores. Data moves between devices by JAX's collectives and lax.ppermute only.
A program may use at most 192 MiB of HBM per device.

v0:
```python
import jax
import jax.numpy as jnp
from jax import lax
from jax.sharding import PartitionSpec as P

PROTOS = 65536
ITERS = 3


TEACHER_TEMP = 0.07
STUDENT_TEMP = 0.1


def normalize_columns(balance):
    column_sum = lax.psum(jnp.sum(balance, axis=0), "batch")
    return balance / column_sum[None, :]


def crop_totals(balance):
    return lax.psum(jnp.sum(balance, axis=1), "proto")


def local(features, head_weight, student_scores):
    gathered = lax.all_gather(features, "proto", axis=0, tiled=True)
    feat_wide = gathered.astype(jnp.float32)
    fnorm = jnp.sqrt(jnp.sum(feat_wide * feat_wide, axis=1) + 1e-06)
    piece = lax.all_gather(head_weight, "batch", axis=0, tiled=True)
    piece_wide = piece.astype(jnp.float32)
    raw = jnp.dot(gathered, piece, preferred_element_type=jnp.float32)
    squares = jnp.sum(piece_wide * piece_wide, axis=0)
    wnorm = jnp.sqrt(squares + 1e-06)
    balance = jnp.exp(raw / (fnorm[:, None] * wnorm[None, :]) / TEACHER_TEMP)
    logits = student_scores.astype(jnp.float32) / STUDENT_TEMP
    exp_sums = jnp.sum(jnp.exp(logits), axis=2)
    for step in range(ITERS - 1):
        balance = normalize_columns(balance)
        balance = balance / crop_totals(balance)[:, None]
    balance = normalize_columns(balance)
    weighted = jnp.sum(logits * balance[None, :, :], axis=2)
    last_rows, total_exp, total_weighted = lax.psum(
        (jnp.sum(balance, axis=1), exp_sums, weighted), "proto"
    )
    balance = balance / last_rows[:, None]
    row_loss = jnp.log(total_exp) - total_weighted / last_rows[None, :]
    targets = (balance * PROTOS).astype(jnp.bfloat16)
    return (targets, row_loss)


def solution(mesh):
    return jax.shard_map(
        local,
        mesh=mesh,
        in_specs=(P(("batch", "proto"), None), P("batch", "proto"), P(None, "batch", "proto")),
        out_specs=(P("batch", "proto"), P(None, "batch")),
        check_vma=False,
    )
```

profile of v0, /device:TPU:0, one launch (start us, length us, event | category | flops | bytes accessed | tf_op | source)
XLA Modules:
  0.0 311.4 jit_solution(16653263350034114309)
XLA Ops:
  7.2 0.0 all-gather.2.cloned.1.call-start
  7.2 0.7 all-gather.2.cloned.1.call-update
  7.9 33.2 %all_gather.6 = bf16[1024,256]{1,0:T(8,128)(2,1)S(1)} all-gather(bf16[128,256]{1,0:T(8,128)(2,1)} %param.3), channel_id=1, replica_groups=mesh['batch'=4,'proto'=8] {'proto'}, dimensions={0}, use_global_device_ids=true | all-gather | bytes 589824 | tf_op jit(solution)/shard_map/all_gather | solution.py:24
  41.1 0.2 multiply_reduce_fusion.1
  41.4 5.4 %all-gather.2.cloned.1.call-done = bf16[256,8192]{1,0:T(8,128)(2,1)} async-done(((bf16[64,8192]{1,0:T(8,128)(2,1)}), bf16[256,8192]{1,0:T(8,128)(2,1)}) %all-gather.2.cloned.1.call-update) | async-done | bytes 4194320 | tf_op jit(solution)/shard_map/all_gather | solution.py:27
  46.7 3.1 multiply_reduce_fusion
  49.8 17.7 %fusion.16 = (f32[8192]{0:T(1024)S(1)}, f32[1024,8192]{1,0:T(8,128)}) fusion(f32[8192]{0:T(1024)S(1)} %add_sqrt_fusion, f32[1024]{0:T(1024)S(1)} %add_sqrt_fusion.1, bf16[1024,256]{1,0:T(8,128)(2,1)S(1)} %all_gather.6, bf16[256,8192]{1,0:T(8,128)(2,1)} %all-gather.2.cloned.1.call-done), kind=kOutput, calls=%fused_computation.28 | convolution fusion | flops 4328513536 | bytes 38342656 | tf_op jit(solution)/shard_map/dot_general | solution.py:29
  67.5 10.4 %psum.56 = f32[8192]{0:T(1024)S(1)} all-reduce(f32[8192]{0:T(1024)S(1)} %get-tuple-element.9), channel_id=1, replica_groups=mesh['batch'=4,'proto'=8] {'batch'}, use_global_device_ids=true, to_apply=%region_3.0 | all-reduce | flops 8192 | bytes 65536 | tf_op jit(solution)/shard_map/psum | solution.py:15
  77.9 12.2 %divide_reduce_fusion = f32[1024]{0:T(1024)S(1)} fusion(f32[1024,8192]{1,0:T(8,128)} %get-tuple-element.10, f32[8192]{0:T(1024)S(1)} %psum.56), kind=kLoop, calls=%fused_computation.16 | loop fusion | flops 16776192 | bytes 33591296 | tf_op jit(solution)/shard_map/reduce_sum | solution.py:20
  90.1 21.5 %psum.57 = f32[1024]{0:T(1024)S(1)} all-reduce(f32[1024]{0:T(1024)S(1)} %divide_reduce_fusion), channel_id=1, replica_groups=mesh['batch'=4,'proto'=8] {'proto'}, use_global_device_ids=true, to_apply=%region_5.0 | all-reduce | flops 1024 | bytes 8192 | tf_op jit(solution)/shard_map/psum | solution.py:20
  111.6 14.1 %fusion.11 = f32[8192]{0:T(1024)S(1)} fusion(f32[1024,8192]{1,0:T(8,128)} %get-tuple-element.10, f32[1024]{0:T(1024)S(1)} %psum.57, f32[8192]{0:T(1024)S(1)} %psum.56), kind=kLoop, calls=%fused_computation.17 | loop fusion | flops 25157632 | bytes 33624064 | tf_op jit(solution)/shard_map/reduce_sum | solution.py:15
  125.7 10.3 %psum.58 = f32[8192]{0:T(1024)S(1)} all-reduce(f32[8192]{0:T(1024)S(1)} %fusion.11), channel_id=1, replica_groups=mesh['batch'=4,'proto'=8] {'batch'}, use_global_device_ids=true, to_apply=%region_7.0 | all-reduce | flops 8192 | bytes 65536 | tf_op jit(solution)/shard_map/psum | solution.py:15
  136.0 14.1 %fusion.13 = f32[1024]{0:T(1024)S(1)} fusion(f32[1024,8192]{1,0:T(8,128)} %get-tuple-element.10, f32[8192]{0:T(1024)S(1)} %psum.58, f32[1024]{0:T(1024)S(1)} %psum.57, f32[8192]{0:T(1024)S(1)} %psum.56), kind=kLoop, calls=%fused_computation.19 | loop fusion | flops 33553408 | bytes 33628160 | tf_op jit(solution)/shard_map/reduce_sum | solution.py:20
  150.1 17.1 %psum.59 = f32[1024]{0:T(1024)S(1)} all-reduce(f32[1024]{0:T(1024)S(1)} %fusion.13), channel_id=1, replica_groups=mesh['batch'=4,'proto'=8] {'proto'}, use_global_device_ids=true, to_apply=%region_9.0 | all-reduce | flops 1024 | bytes 8192 | tf_op jit(solution)/shard_map/psum | solution.py:20
  167.3 14.5 %fusion.14 = f32[8192]{0:T(1024)S(1)} fusion(f32[1024,8192]{1,0:T(8,128)} %get-tuple-element.10, f32[1024]{0:T(1024)S(1)} %psum.59, f32[8192]{0:T(1024)S(1)} %psum.58, f32[1024]{0:T(1024)S(1)} %psum.57, f32[8192]{0:T(1024)S(1)} %psum.56), kind=kLoop, calls=%fused_computation.20 | loop fusion | flops 41934848 | bytes 33660928 | tf_op jit(solution)/shard_map/reduce_sum | solution.py:15
  181.7 10.4 %psum.60 = f32[8192]{0:T(1024)S(1)} all-reduce(f32[8192]{0:T(1024)S(1)} %fusion.14), channel_id=1, replica_groups=mesh['batch'=4,'proto'=8] {'batch'}, use_global_device_ids=true, to_apply=%region_11.0 | all-reduce | flops 8192 | bytes 65536 | tf_op jit(solution)/shard_map/psum | solution.py:15
  192.2 28.0 %broadcast_multiply_fusion = (f32[1024,8192]{1,0:T(8,128)}, f32[1024]{0:T(1024)S(1)}) fusion(f32[1024,8192]{1,0:T(8,128)} %get-tuple-element.10, f32[8192]{0:T(1024)S(1)} %psum.60, f32[1024]{0:T(1024)S(1)} %psum.59, f32[8192]{0:T(1024)S(1)} %psum.58, f32[1024]{0:T(1024)S(1)} %psum.57, f32[8192]{0:T(1024)S(1)} %psum.56), kind=kLoop, calls=%fused_computation.21 | loop fusion | flops 58719232 | bytes 67219456 | tf_op jit(solution)/shard_map/mul | solution.py:39
  220.2 27.8 %fusion.1 = (f32[2,1024]{1,0:T(2,128)S(1)}, f32[2,1024]{1,0:T(2,128)S(1)}) fusion(bf16[2,1024,8192]{2,1,0:T(8,128)(2,1)} %param.5, f32[1024,8192]{1,0:T(8,128)} %get-tuple-element.7), kind=kLoop, calls=%fused_computation.3 | loop fusion | flops 83881984 | bytes 67125248 | tf_op jit(solution)/shard_map/reduce_sum | solution.py:34
  248.0 34.9 %all-reduce = (f32[1024]{0:T(1024)S(1)}, f32[2,1024]{1,0:T(2,128)S(1)}, f32[2,1024]{1,0:T(2,128)S(1)}) all-reduce(f32[1024]{0:T(1024)S(1)} %get-tuple-element.8, f32[2,1024]{1,0:T(2,128)S(1)} %get-tuple-element.3, f32[2,1024]{1,0:T(2,128)S(1)} %get-tuple-element.2), channel_id=1, replica_groups=mesh['batch'=4,'proto'=8] {'proto'}, use_global_device_ids=true, to_apply=%region_13.0 | all-reduce | flops 5120 | bytes 40960 | tf_op jit(solution)/shard_map/psum | solution.py:40
  282.9 21.1 %fusion.12 = bf16[1024,8192]{1,0:T(8,128)(2,1)} fusion(f32[1024,8192]{1,0:T(8,128)} %get-tuple-element.10, f32[1024]{0:T(1024)S(1)} %get-tuple-element.4, f32[8192]{0:T(1024)S(1)} %psum.60, f32[1024]{0:T(1024)S(1)} %psum.59, f32[8192]{0:T(1024)S(1)} %psum.58, f32[1024]{0:T(1024)S(1)} %psum.57, f32[8192]{0:T(1024)S(1)} %psum.56), kind=kLoop, calls=%fused_computation.18 | loop fusion | flops 67108864 | bytes 50442240 | tf_op jit(solution)/shard_map/convert_element_type | solution.py:45
  303.9 0.6 divide_subtract_fusion
  (2 shorter events, 0.0 us)
Async XLA Ops:
  7.2 39.6 %all-gather.2.cloned.1.call-start = ((), (), s32[]{:S(2)}) async-start(), calls=%async_computation | async-start | bytes 5242880 | tf_op jit(solution)/shard_map/all_gather | solution.py:27
Sparse Core Ops, SparseCore 0:
  9.5 37.1 all-gather.1
where the time goes:
time: 312 us; the launch traced here: 311 us
  blocking collectives  138 us (44%)
  other arithmetic  136 us (44%)
  matrix products  17.7 us (6%)
  between operations  14.1 us (5%)
  waiting for transfers between devices  6.05 us (2%)
    psum x2, blocking collectives, crop_totals(): return lax.psum(jnp.sum(balance, axis=1), 'proto')  38.7 us
    psum x1, blocking collectives, local(): lax.psum((jnp.sum(balance, axis=1), exp_sums, weighted), 'proto')  34.9 us
    all_gather x1, blocking collectives, local(): gathered = lax.all_gather(features, 'proto', axis=0, tiled=True)  33.2 us
    psum x3, blocking collectives, normalize_columns(): column_sum = lax.psum(jnp.sum(balance, axis=0), 'batch')  31.1 us
    reduce_sum x2, other arithmetic, normalize_columns(): column_sum = lax.psum(jnp.sum(balance, axis=0), 'batch')  28.5 us
    mul x1, other arithmetic, local(): weighted = jnp.sum(logits * balance[None, :, :], axis=2)  28 us
    reduce_sum x1, other arithmetic, local(): exp_sums = jnp.sum(jnp.exp(logits), axis=2)  27.8 us
    reduce_sum x2, other arithmetic, crop_totals(): return lax.psum(jnp.sum(balance, axis=1), 'proto')  26.3 us
  transfers between devices with their start and end apart: 1, of which 1 were waited for; matrix products, arithmetic and copies ran while one was open for 0% of the time, Pallas kernels for 0%

commit v1 on v0

v1 whole, which is shorter than its diff:
```python
import jax
import jax.numpy as jnp
from jax import lax
from jax.experimental import pallas as pl
from jax.experimental.pallas import tpu as pltpu
from jax.sharding import PartitionSpec as P

PROTOS = 65536
TEACHER_TEMP = 0.07
STUDENT_TEMP = 0.1
LOG2E = 1.4426950408889634
LANES = 128
VMEM = pltpu.MemorySpace.VMEM
HI = lax.Precision.HIGHEST


def params(mib, grid=0):
    return pltpu.CompilerParams(
        vmem_limit_bytes=mib << 20,
        dimension_semantics=("arbitrary",) * grid if grid else None,
    )


def whole():
    return pl.BlockSpec(memory_space=VMEM)


def lane_sums(acc):
    ones = jnp.ones((8, LANES), jnp.float32)
    out = lax.dot_general(ones, acc, (((1,), (1,)), ((), ())), precision=HI,
                          preferred_element_type=jnp.float32)
    return out[0:1]


def to_rows(row):
    return jnp.transpose(jnp.broadcast_to(row, (LANES, LANES)))


def student_kernel(scores, out, acc_ref):
    i = pl.program_id(0)
    views, rows, cols = scores.shape
    sub = 16
    scale = jnp.float32(LOG2E / STUDENT_TEMP)
    for v in range(views):
        def body(r, _):
            at = pl.multiple_of(r * sub, sub)
            acc = [jnp.zeros((sub, LANES), jnp.float32) for _ in range(2)]
            for t in range(cols // LANES):
                s = scores[v, pl.ds(at, sub), t * LANES:(t + 1) * LANES].astype(jnp.float32)
                acc[t % 2] = acc[t % 2] + jnp.exp2(s * scale)
            acc_ref[pl.ds(at, sub), :] = acc[0] + acc[1]
            return 0

        lax.fori_loop(0, rows // sub, body, 0)
        out[v, pl.ds(i, 1), :] = lane_sums(acc_ref[...])


def student_sums(scores):
    views, rows, cols = scores.shape
    n = rows // LANES
    return pl.pallas_call(
        student_kernel,
        grid=(n,),
        in_specs=[pl.BlockSpec((views, LANES, cols), lambda i: (0, i, 0))],
        out_specs=pl.BlockSpec((views, n, LANES), lambda i: (0, 0, 0)),
        out_shape=jax.ShapeDtypeStruct((views, n, LANES), jnp.float32),
        scratch_shapes=[pltpu.VMEM((LANES, LANES), jnp.float32)],
        compiler_params=params(10, 1),
        cost_estimate=pl.CostEstimate(flops=views * rows * cols * 4, transcendentals=views * rows * cols,
                                      bytes_accessed=views * rows * cols * 2),
        name="student_exp",
    )(scores)


def kernel_block(nblocks, step, refs):
    feats = refs[0]
    weights = refs[1:1 + nblocks]
    kmat, csum, fscale = refs[1 + nblocks:]
    rows = feats.shape[0]
    cols = csum.shape[1]
    sub = 128

    def norms(r, _):
        at = pl.multiple_of(r * sub, sub)
        f = feats[pl.ds(at, sub), :].astype(jnp.float32)
        total = jnp.sum(f * f, axis=1, keepdims=True)
        fscale[pl.ds(at, sub), :] = jnp.broadcast_to(
            (LOG2E / TEACHER_TEMP) / jnp.sqrt(total + 1e-06), (sub, LANES))
        return 0

    lax.fori_loop(0, rows // sub, norms, 0)

    def block(c, _):
        at = pl.multiple_of(c * step, step)
        w = jnp.concatenate([ref[:, pl.ds(at, step)] for ref in weights], axis=0)
        wide = w.astype(jnp.float32)
        wscale = 1.0 / jnp.sqrt(jnp.sum(wide * wide, axis=0, keepdims=True) + 1e-06)

        def row_block(r, acc):
            rt = pl.multiple_of(r * sub, sub)
            raw = jnp.dot(feats[pl.ds(rt, sub), :], w, preferred_element_type=jnp.float32)
            fs = fscale[pl.ds(rt, sub), :]
            k = jnp.exp2(raw * jnp.concatenate([fs] * (step // LANES), axis=1) * wscale)
            kmat[pl.ds(rt, sub), pl.ds(at, step)] = k
            return acc + jnp.sum(k.reshape(sub // 8, 8, step), axis=0)

        acc = lax.fori_loop(0, rows // sub, row_block, jnp.zeros((8, step), jnp.float32))
        csum[:, pl.ds(at, step)] = jnp.sum(acc, axis=0, keepdims=True)
        return 0

    lax.fori_loop(0, cols // step, block, 0)


def make_kernel(feats, weights):
    rows = feats.shape[0]
    cols = weights[0].shape[1]
    step = 256
    return pl.pallas_call(
        lambda *refs: kernel_block(len(weights), step, refs),
        in_specs=[whole()] * (1 + len(weights)),
        out_specs=(whole(), whole()),
        out_shape=(pltpu.VMEM((rows, cols), jnp.float32), jax.ShapeDtypeStruct((1, cols), jnp.float32)),
        scratch_shapes=[pltpu.VMEM((rows, LANES), jnp.float32)],
        compiler_params=params(4),
        cost_estimate=pl.CostEstimate(flops=2 * rows * cols * feats.shape[1], transcendentals=rows * cols,
                                      bytes_accessed=cols * 512),
        name="teacher_kernel",
    )(feats, *weights)


def row_pass_kernel(n, refs):
    csums, kmats, out, inv, acc_ref = refs[:n], refs[n:2 * n], refs[2 * n], refs[2 * n + 1], refs[2 * n + 2]
    rows, cols = kmats[0].shape
    sub = 32
    for q in range(n):
        inv[:, q * cols:(q + 1) * cols] = 1.0 / csums[q][...]

    def body(r, _):
        at = pl.multiple_of(r * sub, sub)
        acc = [jnp.zeros((sub, LANES), jnp.float32) for _ in range(2)]
        for q in range(n):
            for t in range(cols // LANES):
                v = inv[:, q * cols + t * LANES:q * cols + (t + 1) * LANES]
                acc[t % 2] = acc[t % 2] + kmats[q][pl.ds(at, sub), t * LANES:(t + 1) * LANES] * v
        acc_ref[pl.ds(at, sub), :] = acc[0] + acc[1]
        return 0

    lax.fori_loop(0, rows // sub, body, 0)
    peers = out.shape[0]
    for i in range(rows // LANES):
        total = lane_sums(acc_ref[i * LANES:(i + 1) * LANES, :])
        for p in range(peers):
            out[p, i:i + 1, :] = total


def row_pass(csums, kmats, peers):
    rows, cols = kmats[0].shape
    n = len(kmats)
    return pl.pallas_call(
        lambda *refs: row_pass_kernel(n, refs),
        in_specs=[whole()] * (2 * n),
        out_specs=whole(),
        out_shape=jax.ShapeDtypeStruct((peers, rows // LANES, LANES), jnp.float32),
        scratch_shapes=[pltpu.VMEM((1, n * cols), jnp.float32), pltpu.VMEM((rows, LANES), jnp.float32)],
        compiler_params=params(2),
        name="row_pass",
    )(*csums, *kmats)


def col_pass_kernel(n, refs):
    rsums, kmats, outs, ub = refs[0], refs[1:1 + n], refs[1 + n:1 + 2 * n], refs[1 + 2 * n]
    rows, cols = kmats[0].shape
    u = 1.0 / jnp.sum(rsums[...], axis=0)
    for i in range(rows // LANES):
        ub[i * LANES:(i + 1) * LANES, :] = to_rows(u[i:i + 1, :])
    tiles = 8
    step = tiles * LANES
    unroll = 8
    for q in range(n):
        for c in range(cols // step):
            def body(r, acc):
                acc = list(acc)
                for j in range(unroll):
                    at = pl.multiple_of(r * 8 * unroll + j * 8, 8)
                    scale = ub[pl.ds(at, 8), :]
                    for t in range(tiles):
                        lo = c * step + t * LANES
                        acc[t] = acc[t] + kmats[q][pl.ds(at, 8), lo:lo + LANES] * scale
                return tuple(acc)

            acc = lax.fori_loop(0, rows // (8 * unroll), body,
                                tuple(jnp.zeros((8, LANES), jnp.float32) for _ in range(tiles)))
            for t in range(tiles):
                lo = c * step + t * LANES
                outs[q][:, lo:lo + LANES] = jnp.sum(acc[t], axis=0, keepdims=True)


def col_pass(rsums, kmats):
    rows, cols = kmats[0].shape
    n = len(kmats)
    return pl.pallas_call(
        lambda *refs: col_pass_kernel(n, refs),
        in_specs=[whole()] * (1 + n),
        out_specs=(whole(),) * n,
        out_shape=(jax.ShapeDtypeStruct((1, cols), jnp.float32),) * n,
        scratch_shapes=[pltpu.VMEM((rows, LANES), jnp.float32)],
        compiler_params=params(2),
        name="col_pass",
    )(rsums, *kmats)


def loss_pass_kernel(n, refs):
    scores, esums = refs[0], refs[1]
    csums, kmats = refs[2:2 + n], refs[2 + n:2 + 2 * n]
    out, inv, acc_ref = refs[2 + 2 * n:]
    i = pl.program_id(0)
    views = scores.shape[0]
    cols = kmats[0].shape[1]
    sub = 16

    @pl.when(i == 0)
    def _():
        for q in range(n):
            inv[:, q * cols:(q + 1) * cols] = 1.0 / csums[q][...]
        for v in range(views):
            for p in range(out.shape[0]):
                out[p, 1 + views + v] = esums[v]

    def body(r, _):
        rt = pl.multiple_of(r * sub, sub)
        at = pl.multiple_of(i * LANES + r * sub, sub)
        acc = [jnp.zeros((sub, LANES), jnp.float32) for _ in range(1 + views)]
        for q in range(n):
            for t in range(cols // LANES):
                lo = q * cols + t * LANES
                k = kmats[q][pl.ds(at, sub), t * LANES:(t + 1) * LANES] * inv[:, lo:lo + LANES]
                acc[0] = acc[0] + k
                for v in range(views):
                    s = scores[v, pl.ds(rt, sub), lo:lo + LANES].astype(jnp.float32)
                    acc[1 + v] = acc[1 + v] + k * s
        for m in range(1 + views):
            acc_ref[m, pl.ds(rt, sub), :] = acc[m]
        return 0

    lax.fori_loop(0, LANES // sub, body, 0)
    for m in range(1 + views):
        total = lane_sums(acc_ref[m])
        for p in range(out.shape[0]):
            out[p, m, pl.ds(i, 1), :] = total


def loss_pass(scores, esums, csums, kmats, peers):
    views, rows, cols = scores.shape
    n = len(kmats)
    nb = rows // LANES
    return pl.pallas_call(
        lambda *refs: loss_pass_kernel(n, refs),
        grid=(nb,),
        in_specs=[pl.BlockSpec((views, LANES, cols), lambda i: (0, i, 0))] + [whole()] * (1 + 2 * n),
        out_specs=pl.BlockSpec((peers, 1 + 2 * views, nb, LANES), lambda i: (0, 0, 0, 0)),
        out_shape=jax.ShapeDtypeStruct((peers, 1 + 2 * views, nb, LANES), jnp.float32),
        scratch_shapes=[pltpu.VMEM((1, cols), jnp.float32), pltpu.VMEM((1 + views, LANES, LANES), jnp.float32)],
        compiler_params=params(10, 1),
        name="loss_pass",
    )(scores, esums, *csums, *kmats)


def target_kernel(n, refs):
    stats = refs[0]
    csums, kmats = refs[1:1 + n], refs[1 + n:1 + 2 * n]
    out, loss, inv, ub = refs[1 + 2 * n:]
    i = pl.program_id(0)
    cols = kmats[0].shape[1]
    nb = stats.shape[2]
    views = loss.shape[0]
    sub = 16

    @pl.when(i == 0)
    def _():
        for q in range(n):
            inv[:, q * cols:(q + 1) * cols] = 1.0 / csums[q][...]
        total = jnp.sum(stats[...], axis=0)
        u = PROTOS / total[0]
        for b in range(nb):
            ub[b * LANES:(b + 1) * LANES, :] = to_rows(u[b:b + 1, :])
        for v in range(views):
            row = jnp.log(total[1 + views + v]) - total[1 + v] / STUDENT_TEMP / total[0]
            for b in range(nb):
                loss[v:v + 1, b * LANES:(b + 1) * LANES] = row[b:b + 1, :]

    def body(r, _):
        rt = pl.multiple_of(r * sub, sub)
        at = pl.multiple_of(i * LANES + r * sub, sub)
        scale = ub[pl.ds(at, sub), :]
        for q in range(n):
            for t in range(cols // LANES):
                lo = q * cols + t * LANES
                k = kmats[q][pl.ds(at, sub), t * LANES:(t + 1) * LANES] * inv[:, lo:lo + LANES]
                out[pl.ds(rt, sub), lo:lo + LANES] = (k * scale).astype(jnp.bfloat16)
        return 0

    lax.fori_loop(0, LANES // sub, body, 0)


def target_pass(stats, csums, kmats, views):
    rows, cols = kmats[0].shape
    n = len(kmats)
    nb = rows // LANES
    return pl.pallas_call(
        lambda *refs: target_kernel(n, refs),
        grid=(nb,),
        in_specs=[whole()] * (1 + 2 * n),
        out_specs=(pl.BlockSpec((LANES, n * cols), lambda i: (i, 0)),
                   pl.BlockSpec((views, rows), lambda i: (0, 0))),
        out_shape=(jax.ShapeDtypeStruct((rows, n * cols), jnp.bfloat16),
                   jax.ShapeDtypeStruct((views, rows), jnp.float32)),
        scratch_shapes=[pltpu.VMEM((1, n * cols), jnp.float32), pltpu.VMEM((rows, LANES), jnp.float32)],
        compiler_params=params(6, 1),
        name="target_pass",
    )(stats, *csums, *kmats)


def xor_pairs(n, mask):
    return [(i, i ^ mask) for i in range(n)]


def program(nbatch, nproto):
    bits = nbatch.bit_length() - 1
    assert 1 << bits == nbatch
    chunks = 4

    def sum_batch(arrays):
        for b in range(bits):
            pairs = xor_pairs(nbatch, 1 << b)
            arrays = [a + lax.ppermute(a, "batch", pairs) for a in arrays]
        return arrays

    def sum_columns(arrays):
        joined = sum_batch([jnp.concatenate(arrays, axis=1)])[0]
        return jnp.split(joined, len(arrays), axis=1)

    def local(features, head_weight, student_scores):
        student_scores = pltpu.with_memory_space_constraint(student_scores, pltpu.MemorySpace.HBM)
        me = lax.axis_index("batch")
        depth, cols = head_weight.shape
        cc = cols // chunks
        masks = [0]
        parts = [[head_weight[:, q * cc:(q + 1) * cc]] for q in range(chunks)]
        for b in reversed(range(bits)):
            pairs = xor_pairs(nbatch, 1 << b)
            for q in range(chunks):
                parts[q] = parts[q] + [lax.ppermute(w, "batch", pairs) for w in parts[q]]
            masks = masks + [m ^ (1 << b) for m in masks]
        mine = jnp.concatenate(
            [lax.dynamic_slice_in_dim(features, (me ^ m) * depth, depth, 1) for m in masks], axis=1)
        copies = jnp.broadcast_to(mine[None], (nproto,) + mine.shape)
        gathered = lax.all_to_all(copies, "proto", 0, 0).reshape(-1, mine.shape[1])
        esums = student_sums(student_scores)
        gathered, esums = lax.optimization_barrier((gathered, esums))

        kmats, csums = zip(*[make_kernel(gathered, parts[q]) for q in range(chunks)])
        for step in range(2):
            csums = sum_columns(csums)
            rsums = row_pass(csums, kmats, nproto)
            rsums = lax.all_to_all(rsums, "proto", 0, 0)
            csums = col_pass(rsums, kmats)
        csums = sum_columns(csums)
        stats = loss_pass(student_scores, esums, csums, kmats, nproto)
        stats = lax.all_to_all(stats, "proto", 0, 0)
        return target_pass(stats, csums, kmats, student_scores.shape[0])

    return local


def solution(mesh):
    return jax.shard_map(
        program(mesh.shape["batch"], mesh.shape["proto"]),
        mesh=mesh,
        in_specs=(P(("batch", "proto"), None), P("batch", "proto"), P(None, "batch", "proto")),
        out_specs=(P("batch", "proto"), P(None, "batch")),
        check_vma=False,
    )
```

time: 312 us -> 194 us (0.62)
  other arithmetic: 136 us -> 0.32 us
  Pallas kernels: 0 us -> 114 us
  blocking collectives: 138 us -> 31.6 us
  starting transfers between devices: 0.04 us -> 18.2 us
  matrix products: 17.7 us -> 0 us
  between operations: 14.1 us -> 0.92 us
  waiting for transfers between devices: 6.05 us -> 17.8 us
  local copies, waits for them, and re-layouts: 0 us -> 9.91 us
    pallas_call x0 -> x11, Pallas kernels: none -> 114 us  [the longest x4 53.2 us: make_kernel(): pl.pallas_call(lambda *refs: kernel_block(len(weights), step, refs), in_s...]
    psum x6 -> x0, blocking collectives: 105 us -> none  [the longest x2 38.7 us: crop_totals(): return lax.psum(jnp.sum(balance, axis=1), 'proto')]
    reduce_sum x7 -> x0, other arithmetic: 85.9 us -> none  [the longest x2 28.5 us: normalize_columns(): column_sum = lax.psum(jnp.sum(balance, axis=0), 'batch')]
    all_gather x1 -> x0, blocking collectives: 33.2 us -> none  [local(): gathered = lax.all_gather(features, 'proto', axis=0, tiled=True)]
    all_to_all x0 -> x3, blocking collectives: none -> 31.6 us  [the longest x2 21.6 us: local(): rsums = lax.all_to_all(rsums, 'proto', 0, 0)]
    mul x1 -> x0, other arithmetic: 28 us -> none  [local(): weighted = jnp.sum(logits * balance[None, :, :], axis=2)]
    convert_element_type x1 -> x0, other arithmetic: 21.1 us -> none  [local(): targets = (balance * PROTOS).astype(jnp.bfloat16)]
    ppermute x0 -> x18, waiting for transfers between devices: none -> 17.8 us  [the longest x6 10.6 us: sum_batch(): arrays = [a + lax.ppermute(a, 'batch', pairs) for a in arrays]]
  transfers between devices with their start and end apart: 1 -> 19, of which waited for: 1 -> 7; matrix products, arithmetic and copies ran while one was open for 0% -> 1% of each run, Pallas kernels for 0% -> 30%
where the time goes in v1:
time: 194 us; the launch traced here: 193 us
  Pallas kernels  114 us (59%)
  blocking collectives  31.6 us (16%)
  starting transfers between devices  18.2 us (9%)
  waiting for transfers between devices  17.8 us (9%)
  local copies, waits for them, and re-layouts  9.91 us (5%)
    pallas_call x4, Pallas kernels, make_kernel(): pl.pallas_call(lambda *refs: kernel_block(len(weights), step, refs), in_s...  53.2 us
    all_to_all x2, blocking collectives, local(): rsums = lax.all_to_all(rsums, 'proto', 0, 0)  21.6 us
    pallas_call x1, Pallas kernels, loss_pass(): pl.pallas_call(lambda *refs: loss_pass_kernel(n, refs), grid=(nb,), in_sp...  19.1 us
    pallas_call x1, Pallas kernels, student_sums(): pl.pallas_call(student_kernel, grid=(n,), in_specs=[pl.BlockSpec((views,...  18.5 us
    ppermute x6, waiting for transfers between devices, sum_batch(): arrays = [a + lax.ppermute(a, 'batch', pairs) for a in arrays]  10.6 us
    all_to_all x1, blocking collectives, local(): stats = lax.all_to_all(stats, 'proto', 0, 0)  9.98 us
    pallas_call x2, Pallas kernels, row_pass(): pl.pallas_call(lambda *refs: row_pass_kernel(n, refs), in_specs=[whole()]...  9.16 us
    pallas_call x1, Pallas kernels, target_pass(): pl.pallas_call(lambda *refs: target_kernel(n, refs), grid=(nb,), in_specs...  8.41 us
  transfers between devices with their start and end apart: 19, of which 7 were waited for; matrix products, arithmetic and copies ran while one was open for 1% of the time, Pallas kernels for 30%

profile of v1, /device:TPU:0, one launch (start us, length us, event | category | flops | bytes accessed | tf_op | source)
XLA Modules:
  0.0 193.2 jit_solution(17814556160314398997)
XLA Ops:
  2.5 7.3 %all-to-all-start = ((bf16[8,128,256]{2,1,0:T(8,128)(2,1)}), bf16[8,128,256]{2,1,0:T(8,128)(2,1)S(1)}, u32[]{:S(2)}, u32[]{:S(2)}) async-start(bf16[8,128,256]{2,1,0:T(8,128)(2,1)} %broadcast_in_dim.2), calls=%async_computation | async-start | bytes 1048576 | tf_op jit(solution)/shard_map/all_to_all | solution.py:357
  11.1 1.6 collective-permute-start
  13.2 7.1 %collective-permute-done.refs_2_ = bf16[64,2048]{1,0:T(8,128)(2,1)S(1)} collective-permute-done((bf16[64,2048]{1,0:T(8,128)(2,1)S(1)}, bf16[64,2048]{1,0:T(8,128)(2,1)S(1)}, u32[]{:S(2)}, u32[]{:S(2)}) %collective-permute-start) | collective-permute-done | bytes 262176 | tf_op jit(solution)/shard_map/ppermute | solution.py:352
  22.4 18.5 %student_exp.1.refs_1_ = f32[2,8,128]{2,1,0:T(8,128)S(1)} custom-call(bf16[2,1024,8192]{2,1,0:T(8,128)(2,1)} %refs_0_.1), custom_call_target="tpu_custom_call" | custom-call | flops 67108864 | bytes 33554432 | tf_op jit(solution)/shard_map/student_exp/pallas_call | solution.py:61
  41.6 13.3 %teacher_kernel.4 = (f32[1024,2048]{1,0:T(8,128)S(1)}, f32[1,2048]{1,0:T(1,128)S(1)}) custom-call(bf16[1024,256]{1,0:T(8,128)(2,1)S(1)} %bitcast.1, bf16[64,2048]{1,0:T(8,128)(2,1)S(1)} %get-tuple-element.40.refs_1_, bf16[64,2048]{1,0:T(8,128)(2,1)S(1)} %collective-permute-done.refs_2_, bf16[64,2048]{1,0:T(8,128)(2,1)S(1)} %collective-permute-done.1.refs_3_, ...), custom_call_target="tpu_custom_call" | custom-call | flops 1073741824 | bytes 1048576 | tf_op jit(solution)/shard_map/teacher_kernel/pallas_call | solution.py:118
  55.9 13.3 %teacher_kernel.5 = (f32[1024,2048]{1,0:T(8,128)S(1)}, f32[1,2048]{1,0:T(1,128)S(1)}) custom-call(bf16[1024,256]{1,0:T(8,128)(2,1)S(1)} %bitcast.2, bf16[64,2048]{1,0:T(8,128)(2,1)S(1)} %get-tuple-element.39.refs_1_, bf16[64,2048]{1,0:T(8,128)(2,1)S(1)} %collective-permute-done.3.refs_2_, bf16[64,2048]{1,0:T(8,128)(2,1)S(1)} %collective-permute-done.4.refs_3_, ...), custom_call_target="tpu_custom_call" | custom-call | flops 1073741824 | bytes 1048576 | tf_op jit(solution)/shard_map/teacher_kernel/pallas_call | solution.py:118
  69.2 13.3 %teacher_kernel.6 = (f32[1024,2048]{1,0:T(8,128)S(1)}, f32[1,2048]{1,0:T(1,128)S(1)}) custom-call(bf16[1024,256]{1,0:T(8,128)(2,1)S(1)} %bitcast.3, bf16[64,2048]{1,0:T(8,128)(2,1)S(1)} %get-tuple-element.41.refs_1_, bf16[64,2048]{1,0:T(8,128)(2,1)S(1)} %collective-permute-done.6.refs_2_, bf16[64,2048]{1,0:T(8,128)(2,1)S(1)} %collective-permute-done.7.refs_3_, ...), custom_call_target="tpu_custom_call" | custom-call | flops 1073741824 | bytes 1048576 | tf_op jit(solution)/shard_map/teacher_kernel/pallas_call | solution.py:118
  82.6 13.3 %teacher_kernel.7 = (f32[1024,2048]{1,0:T(8,128)S(1)}, f32[1,2048]{1,0:T(1,128)S(1)}) custom-call(bf16[1024,256]{1,0:T(8,128)(2,1)S(1)} %bitcast.4, bf16[64,2048]{1,0:T(8,128)(2,1)S(1)} %get-tuple-element.38.refs_1_, bf16[64,2048]{1,0:T(8,128)(2,1)S(1)} %collective-permute-done.9.refs_2_, bf16[64,2048]{1,0:T(8,128)(2,1)S(1)} %collective-permute-done.10.refs_3_, ...), custom_call_target="tpu_custom_call" | custom-call | flops 1073741824 | bytes 1048576 | tf_op jit(solution)/shard_map/teacher_kernel/pallas_call | solution.py:118
  97.2 1.6 collective-permute-start.13
  98.8 2.4 %collective-permute-done.13 = f32[1,8192]{1,0:T(1,128)S(1)} collective-permute-done((f32[1,8192]{1,0:T(1,128)S(1)}, f32[1,8192]{1,0:T(1,128)S(1)}, u32[]{:S(2)}, u32[]{:S(2)}) %collective-permute-start.13) | collective-permute-done | bytes 32800 | tf_op jit(solution)/shard_map/ppermute | solution.py:335
  101.3 4.6 %row_pass.2 = f32[8,8,128]{2,1,0:T(8,128)S(1)} custom-call(f32[1,2048]{1,0:T(1,128)S(1)} %get-tuple-element.57.refs_0_, f32[1,2048]{1,0:T(1,128)S(1)} %get-tuple-element.56.refs_1_, f32[1,2048]{1,0:T(1,128)S(1)} %get-tuple-element.55.refs_2_, f32[1,2048]{1,0:T(1,128)S(1)} %get-tuple-element.54.refs_3_, ...), custom_call_target="tpu_custom_call" | custom-call | tf_op jit(solution)/shard_map/row_pass/pallas_call | solution.py:159
  105.8 12.5 %all_to_all.20.refs_0_ = f32[8,8,128]{2,1,0:T(8,128)S(1)} all-to-all(f32[8,8,128]{2,1,0:T(8,128)S(1)} %row_pass.2), channel_id=1, replica_groups=mesh['batch'=4,'proto'=8] {'proto'}, dimensions={0} | all-to-all | bytes 65536 | tf_op jit(solution)/shard_map/all_to_all | solution.py:365
  118.3 3.1 %col_pass.2 = (f32[1,2048]{1,0:T(1,128)S(1)}, f32[1,2048]{1,0:T(1,128)S(1)}, f32[1,2048]{1,0:T(1,128)S(1)}, f32[1,2048]{1,0:T(1,128)S(1)}) custom-call(f32[8,8,128]{2,1,0:T(8,128)S(1)} %all_to_all.20.refs_0_, f32[1024,2048]{1,0:T(8,128)S(1)} %get-tuple-element.26.refs_4_.refs_1_.refs_6_.refs_5_, ...), custom_call_target="tpu_custom_call" | custom-call | tf_op jit(solution)/shard_map/col_pass/pallas_call | solution.py:201
  122.8 1.6 collective-permute-start.15
  124.4 2.4 %collective-permute-done.15 = f32[1,8192]{1,0:T(1,128)S(1)} collective-permute-done((f32[1,8192]{1,0:T(1,128)S(1)}, f32[1,8192]{1,0:T(1,128)S(1)}, u32[]{:S(2)}, u32[]{:S(2)}) %collective-permute-start.15) | collective-permute-done | bytes 32800 | tf_op jit(solution)/shard_map/ppermute | solution.py:335
  126.8 4.6 %row_pass.3 = f32[8,8,128]{2,1,0:T(8,128)S(1)} custom-call(f32[1,2048]{1,0:T(1,128)S(1)} %get-tuple-element.53.refs_0_, f32[1,2048]{1,0:T(1,128)S(1)} %get-tuple-element.52.refs_1_, f32[1,2048]{1,0:T(1,128)S(1)} %get-tuple-element.51.refs_2_, f32[1,2048]{1,0:T(1,128)S(1)} %get-tuple-element.50.refs_3_, ...), custom_call_target="tpu_custom_call" | custom-call | tf_op jit(solution)/shard_map/row_pass/pallas_call | solution.py:159
  131.4 9.1 %all_to_all.21.refs_0_ = f32[8,8,128]{2,1,0:T(8,128)S(1)} all-to-all(f32[8,8,128]{2,1,0:T(8,128)S(1)} %row_pass.3), channel_id=1, replica_groups=mesh['batch'=4,'proto'=8] {'proto'}, dimensions={0} | all-to-all | bytes 65536 | tf_op jit(solution)/shard_map/all_to_all | solution.py:365
  140.5 3.1 %col_pass.3 = (f32[1,2048]{1,0:T(1,128)S(1)}, f32[1,2048]{1,0:T(1,128)S(1)}, f32[1,2048]{1,0:T(1,128)S(1)}, f32[1,2048]{1,0:T(1,128)S(1)}) custom-call(f32[8,8,128]{2,1,0:T(8,128)S(1)} %all_to_all.21.refs_0_, f32[1024,2048]{1,0:T(8,128)S(1)} %get-tuple-element.26.refs_4_.refs_1_.refs_6_.refs_5_, ...), custom_call_target="tpu_custom_call" | custom-call | tf_op jit(solution)/shard_map/col_pass/pallas_call | solution.py:201
  146.5 2.4 %collective-permute-done.17 = f32[1,8192]{1,0:T(1,128)S(1)} collective-permute-done((f32[1,8192]{1,0:T(1,128)S(1)}, f32[1,8192]{1,0:T(1,128)S(1)}, u32[]{:S(2)}, u32[]{:S(2)}) %collective-permute-start.17) | collective-permute-done | bytes 32800 | tf_op jit(solution)/shard_map/ppermute | solution.py:335
  149.0 3.4 %copy-done.1 = f32[1024,2048]{1,0:T(8,128)S(1)} copy-done((f32[1024,2048]{1,0:T(8,128)S(1)}, f32[1024,2048]{1,0:T(8,128)}, u32[]{:S(2)}) %copy-start.1) | copy-done | bytes 8388632
  152.4 3.4 %copy-done.3 = f32[1024,2048]{1,0:T(8,128)S(1)} copy-done((f32[1024,2048]{1,0:T(8,128)S(1)}, f32[1024,2048]{1,0:T(8,128)}, u32[]{:S(2)}) %copy-start.3) | copy-done | bytes 8388632
  155.7 19.1 %loss_pass.1 = f32[8,5,8,128]{3,2,1,0:T(8,128)S(1)} custom-call(bf16[2,1024,8192]{2,1,0:T(8,128)(2,1)} %refs_0_.1, f32[2,8,128]{2,1,0:T(8,128)S(1)} %student_exp.1.refs_1_, f32[1,2048]{1,0:T(1,128)S(1)} %get-tuple-element.49.refs_2_.refs_1_, f32[1,2048]{1,0:T(1,128)S(1)} %get-tuple-element.48.refs_3_.refs_2_, ...), custom_call_target="tpu_custom_call" | custom-call | tf_op jit(solution)/shard_map/loss_pass/pallas_call | solution.py:256
  174.8 10.0 %all_to_all.22.refs_0_ = f32[8,5,8,128]{3,2,1,0:T(8,128)S(1)} all-to-all(f32[8,5,8,128]{3,2,1,0:T(8,128)S(1)} %loss_pass.1), channel_id=1, replica_groups=mesh['batch'=4,'proto'=8] {'proto'}, dimensions={0} | all-to-all | bytes 327680 | tf_op jit(solution)/shard_map/all_to_all | solution.py:369
  184.8 8.4 %target_pass.1 = (bf16[1024,8192]{1,0:T(8,128)(2,1)}, f32[2,1024]{1,0:T(2,128)}) custom-call(f32[8,5,8,128]{3,2,1,0:T(8,128)S(1)} %all_to_all.22.refs_0_, f32[1,2048]{1,0:T(1,128)S(1)} %get-tuple-element.49.refs_2_.refs_1_, f32[1,2048]{1,0:T(1,128)S(1)} %get-tuple-element.48.refs_3_.refs_2_, f32[1,2048]{1,0:T(1,128)S(1)} %get-tuple-element.47.refs_4_.refs_3_, ...), custom_call_target="tpu_custom_call" | custom-call | tf_op jit(solution)/shard_map/target_pass/pallas_call | solution.py:309
  (61 shorter events, 13.1 us)
Async XLA Ops:
  2.5 38.3 %all-to-all-start = ((bf16[8,128,256]{2,1,0:T(8,128)(2,1)}), bf16[8,128,256]{2,1,0:T(8,128)(2,1)S(1)}, u32[]{:S(2)}, u32[]{:S(2)}) async-start(bf16[8,128,256]{2,1,0:T(8,128)(2,1)} %broadcast_in_dim.2), calls=%async_computation | async-start | bytes 1048576 | tf_op jit(solution)/shard_map/all_to_all | solution.py:357
  11.1 9.2 %collective-permute-start = (bf16[64,2048]{1,0:T(8,128)(2,1)S(1)}, bf16[64,2048]{1,0:T(8,128)(2,1)S(1)}, u32[]{:S(2)}, u32[]{:S(2)}) collective-permute-start(bf16[64,2048]{1,0:T(8,128)(2,1)S(1)} %get-tuple-element.40.refs_1_), channel_id=1, source_target_pairs={{0,16},{8,24},{16,0},{24,8},{1,17},{9,25},{17,1},{25,9},{2,18},{10... | collective-permute-start | bytes 786440 | tf_op jit(solution)/shard_map/ppermute | solution.py:352
  12.7 28.1 %collective-permute-start.3 = (bf16[64,2048]{1,0:T(8,128)(2,1)S(1)}, bf16[64,2048]{1,0:T(8,128)(2,1)S(1)}, u32[]{:S(2)}, u32[]{:S(2)}) collective-permute-start(bf16[64,2048]{1,0:T(8,128)(2,1)S(1)} %get-tuple-element.39.refs_1_), channel_id=1, source_target_pairs={{0,16},{8,24},{16,0},{24,8},{1,17},{9,25},{17,1},{25,9},{2,18},{10... | collective-permute-start | bytes 786440 | tf_op jit(solution)/shard_map/ppermute | solution.py:352
  13.2 27.7 %collective-permute-start.1 = (bf16[64,2048]{1,0:T(8,128)(2,1)S(1)}, bf16[64,2048]{1,0:T(8,128)(2,1)S(1)}, u32[]{:S(2)}, u32[]{:S(2)}) collective-permute-start(bf16[64,2048]{1,0:T(8,128)(2,1)S(1)} %get-tuple-element.40.refs_1_), channel_id=1, source_target_pairs={{0,8},{8,0},{16,24},{24,16},{1,9},{9,1},{17,25},{25,17},{2,10},{10... | collective-permute-start | bytes 786440 | tf_op jit(solution)/shard_map/ppermute | solution.py:352
  20.3 21.1 %collective-permute-start.2 = (bf16[64,2048]{1,0:T(8,128)(2,1)S(1)}, bf16[64,2048]{1,0:T(8,128)(2,1)S(1)}, u32[]{:S(2)}, u32[]{:S(2)}) collective-permute-start(bf16[64,2048]{1,0:T(8,128)(2,1)S(1)} %collective-permute-done.refs_2_), channel_id=1, source_target_pairs={{0,8},{8,0},{16,24},{24,16},{1,9},{9,1},{17,25},{25,17},{2,10},{10... | collective-permute-start | bytes 786440 | tf_op jit(solution)/shard_map/ppermute | solution.py:352
  20.3 62.2 %collective-permute-start.10 = (bf16[64,2048]{1,0:T(8,128)(2,1)S(1)}, bf16[64,2048]{1,0:T(8,128)(2,1)S(1)}, u32[]{:S(2)}, u32[]{:S(2)}) collective-permute-start(bf16[64,2048]{1,0:T(8,128)(2,1)S(1)} %get-tuple-element.38.refs_1_), channel_id=1, source_target_pairs={{0,8},{8,0},{16,24},{24,16},{1,9},{9,1},{17,25},{25,17},{2,10},{10... | collective-permute-start | bytes 786440 | tf_op jit(solution)/shard_map/ppermute | solution.py:352
  20.8 34.1 %collective-permute-start.9 = (bf16[64,2048]{1,0:T(8,128)(2,1)S(1)}, bf16[64,2048]{1,0:T(8,128)(2,1)S(1)}, u32[]{:S(2)}, u32[]{:S(2)}) collective-permute-start(bf16[64,2048]{1,0:T(8,128)(2,1)S(1)} %get-tuple-element.38.refs_1_), channel_id=1, source_target_pairs={{0,16},{8,24},{16,0},{24,8},{1,17},{9,25},{17,1},{25,9},{2,18},{10... | collective-permute-start | bytes 786440 | tf_op jit(solution)/shard_map/ppermute | solution.py:352
  40.8 14.6 %collective-permute-start.4 = (bf16[64,2048]{1,0:T(8,128)(2,1)S(1)}, bf16[64,2048]{1,0:T(8,128)(2,1)S(1)}, u32[]{:S(2)}, u32[]{:S(2)}) collective-permute-start(bf16[64,2048]{1,0:T(8,128)(2,1)S(1)} %get-tuple-element.39.refs_1_), channel_id=1, source_target_pairs={{0,8},{8,0},{16,24},{24,16},{1,9},{9,1},{17,25},{25,17},{2,10},{10... | collective-permute-start | bytes 786440 | tf_op jit(solution)/shard_map/ppermute | solution.py:352
  40.9 14.6 %collective-permute-start.6 = (bf16[64,2048]{1,0:T(8,128)(2,1)S(1)}, bf16[64,2048]{1,0:T(8,128)(2,1)S(1)}, u32[]{:S(2)}, u32[]{:S(2)}) collective-permute-start(bf16[64,2048]{1,0:T(8,128)(2,1)S(1)} %get-tuple-element.41.refs_1_), channel_id=1, source_target_pairs={{0,16},{8,24},{16,0},{24,8},{1,17},{9,25},{17,1},{25,9},{2,18},{10... | collective-permute-start | bytes 786440 | tf_op jit(solution)/shard_map/ppermute | solution.py:352
  41.5 14.4 %collective-permute-start.5 = (bf16[64,2048]{1,0:T(8,128)(2,1)S(1)}, bf16[64,2048]{1,0:T(8,128)(2,1)S(1)}, u32[]{:S(2)}, u32[]{:S(2)}) collective-permute-start(bf16[64,2048]{1,0:T(8,128)(2,1)S(1)} %collective-permute-done.3.refs_2_), channel_id=1, source_target_pairs={{0,8},{8,0},{16,24},{24,16},{1,9},{9,1},{17,25},{25,17},{2,10},{10... | collective-permute-start | bytes 786440 | tf_op jit(solution)/shard_map/ppermute | solution.py:352
  54.9 14.3 %collective-permute-start.7 = (bf16[64,2048]{1,0:T(8,128)(2,1)S(1)}, bf16[64,2048]{1,0:T(8,128)(2,1)S(1)}, u32[]{:S(2)}, u32[]{:S(2)}) collective-permute-start(bf16[64,2048]{1,0:T(8,128)(2,1)S(1)} %get-tuple-element.41.refs_1_), channel_id=1, source_target_pairs={{0,8},{8,0},{16,24},{24,16},{1,9},{9,1},{17,25},{25,17},{2,10},{10... | collective-permute-start | bytes 786440 | tf_op jit(solution)/shard_map/ppermute | solution.py:352
  55.4 27.2 %collective-permute-start.11 = (bf16[64,2048]{1,0:T(8,128)(2,1)S(1)}, bf16[64,2048]{1,0:T(8,128)(2,1)S(1)}, u32[]{:S(2)}, u32[]{:S(2)}) collective-permute-start(bf16[64,2048]{1,0:T(8,128)(2,1)S(1)} %collective-permute-done.9.refs_2_), channel_id=1, source_target_pairs={{0,8},{8,0},{16,24},{24,16},{1,9},{9,1},{17,25},{25,17},{2,10},{10... | collective-permute-start | bytes 786440 | tf_op jit(solution)/shard_map/ppermute | solution.py:352
  55.5 13.7 %collective-permute-start.8 = (bf16[64,2048]{1,0:T(8,128)(2,1)S(1)}, bf16[64,2048]{1,0:T(8,128)(2,1)S(1)}, u32[]{:S(2)}, u32[]{:S(2)}) collective-permute-start(bf16[64,2048]{1,0:T(8,128)(2,1)S(1)} %collective-permute-done.6.refs_2_), channel_id=1, source_target_pairs={{0,8},{8,0},{16,24},{24,16},{1,9},{9,1},{17,25},{25,17},{2,10},{10... | collective-permute-start | bytes 786440 | tf_op jit(solution)/shard_map/ppermute | solution.py:352
  82.5 57.9 %copy-start = (f32[1024,2048]{1,0:T(8,128)}, f32[1024,2048]{1,0:T(8,128)S(1)}, u32[]{:S(2)}) copy-start(f32[1024,2048]{1,0:T(8,128)S(1)} %get-tuple-element.28.refs_6_.refs_3_.refs_8_.refs_7_) | copy-start | bytes 25165828
  95.9 44.6 %copy-start.2 = (f32[1024,2048]{1,0:T(8,128)}, f32[1024,2048]{1,0:T(8,128)S(1)}, u32[]{:S(2)}) copy-start(f32[1024,2048]{1,0:T(8,128)S(1)} %get-tuple-element.29.refs_7_.refs_4_.refs_9_.refs_8_) | copy-start | bytes 25165828
  95.9 1.3 collective-permute-start.12
  97.2 4.0 %collective-permute-start.13 = (f32[1,8192]{1,0:T(1,128)S(1)}, f32[1,8192]{1,0:T(1,128)S(1)}, u32[]{:S(2)}, u32[]{:S(2)}) collective-permute-start(f32[1,8192]{1,0:T(1,128)S(1)} %add.34), channel_id=1, source_target_pairs={{0,16},{8,24},{16,0},{24,8},{1,17},{9,25},{17,1},{25,9},{2,18},{10... | collective-permute-start | bytes 98312 | tf_op jit(solution)/shard_map/ppermute | solution.py:335
  121.5 1.3 collective-permute-start.14
  122.8 4.0 %collective-permute-start.15 = (f32[1,8192]{1,0:T(1,128)S(1)}, f32[1,8192]{1,0:T(1,128)S(1)}, u32[]{:S(2)}, u32[]{:S(2)}) collective-permute-start(f32[1,8192]{1,0:T(1,128)S(1)} %add.36), channel_id=1, source_target_pairs={{0,16},{8,24},{16,0},{24,8},{1,17},{9,25},{17,1},{25,9},{2,18},{10... | collective-permute-start | bytes 98312 | tf_op jit(solution)/shard_map/ppermute | solution.py:335
  143.6 1.3 collective-permute-start.16
  144.9 4.0 %collective-permute-start.17 = (f32[1,8192]{1,0:T(1,128)S(1)}, f32[1,8192]{1,0:T(1,128)S(1)}, u32[]{:S(2)}, u32[]{:S(2)}) collective-permute-start(f32[1,8192]{1,0:T(1,128)S(1)} %add.38), channel_id=1, source_target_pairs={{0,16},{8,24},{16,0},{24,8},{1,17},{9,25},{17,1},{25,9},{2,18},{10... | collective-permute-start | bytes 98312 | tf_op jit(solution)/shard_map/ppermute | solution.py:335
  149.0 3.4 %copy-start.1 = (f32[1024,2048]{1,0:T(8,128)S(1)}, f32[1024,2048]{1,0:T(8,128)}, u32[]{:S(2)}) copy-start(f32[1024,2048]{1,0:T(8,128)} %copy-done) | copy-start | bytes 25165828
  152.4 3.4 %copy-start.3 = (f32[1024,2048]{1,0:T(8,128)S(1)}, f32[1024,2048]{1,0:T(8,128)}, u32[]{:S(2)}) copy-start(f32[1024,2048]{1,0:T(8,128)} %copy-done.2) | copy-start | bytes 25165828
